TPU v7x, 256 devices: a whole 4x4x8 slice. The times are simulated.
256 devices in a mesh: cuts: 8 (over y, core), dom: 32 (over z, x).
Axes of the slice: x: 4, y: 4, z: 8, core: 2. Of those that a mesh axis runs over, the one named last changes fastest.
Arguments:
- feats: bfloat16 [65536, 4096], P('dom', 'cuts'), may hold values from -6 to 6
- adjacency: bfloat16 [2048, 128, 128], P('dom'), may hold values from 0 to 0.024658203
- blk_dst: int32 [2048], P('dom'), may hold values from 0 to 31
- blk_src: int32 [2048], P('dom'), may hold values from 0 to 15
- blk_count: int32 [32], P('dom'), may hold values from 1 to 64, as said below
- nbr_ids: int32 [4096, 8], P('dom'), may hold values from 0 to 4095
- edge_types: int32 [4096, 8], P('dom'), may hold values from 0 to 3
- w_first: bfloat16 [4096, 128], P('cuts'), may hold values from -0.09375 to 0.09375
- w_edge: bfloat16 [128, 512], replicated, may hold values from -0.1875 to 0.1875
- w_gate_in: bfloat16 [128, 384], replicated, may hold values from -0.5 to 0.5
- w_gate_state: bfloat16 [128, 256], replicated, may hold values from -0.5 to 0.5
- w_cand: bfloat16 [128, 128], replicated, may hold values from -0.5 to 0.5
- out_grad: bfloat16 [4096, 128], P('dom'), may hold values from -0.5 to 0.5
Outputs:
- new_state: bfloat16 [4096, 128], P('dom')
- w_first_grad: float32 [4096, 128], P(('cuts', 'dom'))
Inputs may be any that keep to these rules, and one draw needn't show every extreme that they name: `blk_count`: slot b counts for partition b // 64 only if b mod 64 is below this count; the other slots are padding; some partition has all 64 slots live. `blk_dst`: a destination block number. `blk_src`: a source block number within the partition.
All inputs are finite; a program needn't handle non-finite values.
Results may differ from a plain program's by a relative error of at most 0.0075.
Values may be sent and summed in bfloat16 or wider, within the bound.
No kernel may reach another device: no remote copies, remote signals or barrier semaphores. Data moves between devices by JAX's collectives and lax.ppermute only.
A program may use at most 64 MiB of HBM per device.

v0:
```python
import math
import jax
import jax.numpy as jnp
from jax import lax
from jax.sharding import PartitionSpec as P


def edge_messages(states, nbr_ids, edge_types, w_edge):
    row_count, fanout = nbr_ids.shape
    hidden = states.shape[1]
    num_types = w_edge.shape[1] // hidden
    picked = states[nbr_ids.reshape(-1)]
    projected = jnp.dot(picked, w_edge, preferred_element_type=jnp.float32).reshape(
        row_count, fanout, num_types, hidden
    )
    one_hot = (
        edge_types[:, :, None] == jnp.arange(num_types, dtype=jnp.int32)[None, None, :]
    ).astype(jnp.float32)
    return jnp.sum(projected * one_hot[:, :, :, None], axis=(1, 2))


def edge_backward(message_grad, nbr_ids, edge_types, w_edge):
    row_count, fanout = nbr_ids.shape
    hidden = message_grad.shape[1]
    num_types = w_edge.shape[1] // hidden
    w_back = (
        w_edge.reshape(hidden, num_types, hidden)
        .transpose(2, 1, 0)
        .reshape(hidden, num_types * hidden)
    )
    per_type = jnp.dot(message_grad, w_back, preferred_element_type=jnp.float32).reshape(
        row_count, 1, num_types, hidden
    )
    one_hot = (
        edge_types[:, :, None] == jnp.arange(num_types, dtype=jnp.int32)[None, None, :]
    ).astype(jnp.float32)
    return jnp.sum(per_type * one_hot[:, :, :, None], axis=2)


def gated_update(message, states, out_grad, w_gate_in, w_gate_state, w_cand):
    hidden = states.shape[1]
    message_in = message.astype(jnp.bfloat16)
    gate_in = jnp.dot(message_in, w_gate_in, preferred_element_type=jnp.float32)
    gate_state = jnp.dot(states, w_gate_state, preferred_element_type=jnp.float32)
    state_value = states.astype(jnp.float32)
    update = jax.nn.sigmoid(gate_in[:, :hidden] + gate_state[:, :hidden])
    reset = jax.nn.sigmoid(gate_in[:, hidden : 2 * hidden] + gate_state[:, hidden:])
    reset_state = (reset * state_value).astype(jnp.bfloat16)
    candidate = jnp.tanh(
        gate_in[:, 2 * hidden :] + jnp.dot(reset_state, w_cand, preferred_element_type=jnp.float32)
    )
    new_state = ((1.0 - update) * candidate + update * state_value).astype(jnp.bfloat16)
    out_value = out_grad.astype(jnp.float32)
    cand_pre = out_value * (1.0 - update) * (1.0 - candidate * candidate)
    update_pre = out_value * (state_value - candidate) * update * (1.0 - update)
    cand_grad = cand_pre.astype(jnp.bfloat16)
    reset_grad_in = jnp.dot(cand_grad, w_cand.T, preferred_element_type=jnp.float32)
    reset_pre = reset_grad_in * state_value * reset * (1.0 - reset)
    gate_grads = jnp.concatenate([update_pre, reset_pre, cand_pre], axis=1).astype(jnp.bfloat16)
    message_grad = jnp.dot(gate_grads, w_gate_in.T, preferred_element_type=jnp.float32).astype(
        jnp.bfloat16
    )
    state_grad = (
        out_value * update
        + reset_grad_in * reset
        + jnp.dot(gate_grads[:, : 2 * hidden], w_gate_state.T, preferred_element_type=jnp.float32)
    )
    return (new_state, message_grad, state_grad)


def rows_in_window(flat_contrib, flat_targets, rows_wanted):
    inside = (flat_targets >= 0) & (flat_targets < rows_wanted)
    summed = jax.ops.segment_sum(
        jnp.where(inside[:, None], flat_contrib, 0.0),
        jnp.where(inside, flat_targets, rows_wanted),
        num_segments=rows_wanted + 1,
    )
    return summed[:rows_wanted]


def body(
    feats,
    adjacency,
    blk_dst,
    blk_src,
    blk_count,
    nbr_ids,
    edge_types,
    w_first,
    w_edge,
    w_gate_in,
    w_gate_state,
    w_cand,
    out_grad,
):
    block_count = adjacency.shape[0]
    block_rows = adjacency.shape[1]
    feat_cols = feats.shape[1]
    hidden = w_first.shape[1]
    row_count = out_grad.shape[0]
    domains = lax.axis_size("dom")
    total_rows = row_count * domains
    feat_tiles = feats.reshape(-1, block_rows, feat_cols)
    live_mask = jnp.arange(block_count, dtype=jnp.int32) < blk_count[0]
    group_size = math.gcd(block_count, 16)
    groups = block_count // group_size

    def one_group(group):
        adj_group, src_group, live_group = group
        src_rows = feat_tiles[src_group]
        aggregated = jnp.einsum(
            "bij,bjf->bif", adj_group, src_rows, preferred_element_type=jnp.float32
        ).astype(jnp.bfloat16)
        projected = jnp.einsum(
            "bif,fh->bih", aggregated, w_first, preferred_element_type=jnp.float32
        )
        return (aggregated, jnp.where(live_group[:, None, None], projected, 0.0))

    aggregated, projected = lax.map(
        one_group,
        (
            adjacency.reshape(groups, group_size, block_rows, block_rows),
            blk_src.reshape(groups, group_size),
            live_mask.reshape(groups, group_size),
        ),
    )
    aggregated = aggregated.reshape(block_count, block_rows, feat_cols)
    projected = projected.reshape(block_count, block_rows, hidden)
    partial_value = jax.ops.segment_sum(
        projected, blk_dst, num_segments=total_rows // block_rows
    ).reshape(total_rows, hidden)
    owned = lax.psum_scatter(partial_value, "dom", scatter_dimension=0, tiled=True)
    first = lax.psum(owned, "cuts")
    state_exact = jnp.tanh(first)
    states = state_exact.astype(jnp.bfloat16)
    all_states = lax.all_gather(states, "dom", axis=0, tiled=True)
    message = edge_messages(all_states, nbr_ids, edge_types, w_edge)
    new_state, message_grad, state_grad = gated_update(
        message, states, out_grad, w_gate_in, w_gate_state, w_cand
    )
    contrib = edge_backward(message_grad, nbr_ids, edge_types, w_edge)
    flat_contrib = contrib.reshape(-1, hidden)
    flat_targets = nbr_ids.reshape(-1)
    state_grad = state_grad + lax.psum_scatter(
        rows_in_window(flat_contrib, flat_targets, lax.axis_size("dom") * row_count),
        "dom",
        scatter_dimension=0,
        tiled=True,
    )
    first_grad = (state_grad * (1.0 - state_exact * state_exact)).astype(jnp.bfloat16)
    all_grads = lax.all_gather(first_grad, "dom", axis=0, tiled=True)
    picked_grads = jnp.where(
        live_mask[:, None, None],
        all_grads.reshape(-1, block_rows, hidden)[blk_dst],
        jnp.zeros((), jnp.bfloat16),
    )
    w_first_grad = lax.psum_scatter(
        jnp.einsum("bif,bih->fh", aggregated, picked_grads, preferred_element_type=jnp.float32),
        "dom",
        scatter_dimension=0,
        tiled=True,
    )
    return (new_state, w_first_grad)


def solution(mesh):
    return jax.shard_map(
        body,
        mesh=mesh,
        in_specs=(
            P("dom", "cuts"),
            P("dom", None, None),
            P("dom"),
            P("dom"),
            P("dom"),
            P("dom", None),
            P("dom", None),
            P("cuts", None),
            P(),
            P(),
            P(),
            P(),
            P("dom", None),
        ),
        out_specs=(P("dom", None), P(("cuts", "dom"), None)),
        check_vma=False,
    )
```

profile of v0, /device:TPU:8, one launch (start us, length us, event | category | flops | bytes accessed | tf_op | source)
XLA Modules:
  0.0 952.8 jit_solution(16278091829357326232)
XLA Ops:
  8.6 28.6 %while.12 = (s32[]{:T(128)}, bf16[4,16,128,512]{3,2,1,0:T(8,128)(2,1)}, f32[4,16,128,128]{3,2,1,0:T(8,128)}, bf16[4,16,128,128]{3,2,1,0:T(8,128)(2,1)}, s32[4,16...) while((s32[]{:T(128)}, ...), condition=%wide.region_1.2_spmd, body=%wide.region_0.1_spmd.sunk | while | flops 538182720 | bytes 14817201 | solution.py:119
  8.7 2.3 gather_fusion
  11.0 3.1 bitcast_dynamic-update-slice_fusion.2
  14.1 1.8 fusion.95
  15.9 2.3 gather_fusion
  18.1 3.1 bitcast_dynamic-update-slice_fusion.2
  21.3 1.7 fusion.95
  23.0 2.3 gather_fusion
  25.2 3.1 bitcast_dynamic-update-slice_fusion.2
  28.4 1.7 fusion.95
  30.1 2.3 gather_fusion
  32.4 3.1 bitcast_dynamic-update-slice_fusion.2
  35.5 1.7 fusion.95
  37.9 8.8 scatter_fusion
  48.1 221.8 %reduce-scatter.4.cloned.1.call-done = f32[128,128]{1,0:T(8,128)} async-done(((f32[4096,128]{1,0:T(8,128)}), f32[128,128]{1,0:T(8,128)}) %reduce-scatter.4.cloned.1.call-update) | async-done | bytes 65552 | tf_op jit(solution)/shard_map/reduce_scatter | solution.py:132
  270.0 63.2 %all-reduce.2.cloned.1.call-done = f32[128,128]{1,0:T(8,128)} async-done(((f32[128,128]{1,0:T(8,128)}), f32[128,128]{1,0:T(8,128)}) %all-reduce.2.cloned.1.call-update) | async-done | bytes 65552 | tf_op jit(solution)/shard_map/psum | solution.py:133
  336.5 77.3 %all-gather.3.cloned.1.call-done = bf16[4096,128]{1,0:T(8,128)(2,1)} async-done(((bf16[128,128]{1,0:T(8,128)(2,1)}), bf16[4096,128]{1,0:T(8,128)(2,1)}) %all-gather.3.cloned.1.call-update) | async-done | bytes 1048592 | tf_op jit(solution)/shard_map/all_gather | solution.py:136
  413.8 4.2 gather_fusion.1
  421.2 7.1 scatter_custom_fusion.1
  429.9 216.2 %reduce-scatter.6.cloned.1.call-done = f32[128,128]{1,0:T(8,128)} async-done(((f32[4096,128]{1,0:T(8,128)}), f32[128,128]{1,0:T(8,128)}) %reduce-scatter.6.cloned.1.call-update) | async-done | bytes 65552 | tf_op jit(solution)/shard_map/reduce_scatter | solution.py:144
  647.9 75.4 %all-gather.5.cloned.1.call-done = bf16[4096,128]{1,0:T(8,128)(2,1)} async-done(((bf16[128,128]{1,0:T(8,128)(2,1)}), bf16[4096,128]{1,0:T(8,128)(2,1)}) %all-gather.5.cloned.1.call-update) | async-done | bytes 1048592 | tf_op jit(solution)/shard_map/all_gather | solution.py:151
  723.2 2.2 gather_fusion.2
  725.4 6.7 fusion.12
  732.2 213.7 %reduce-scatter.8.cloned.1.call-done = f32[16,128]{1,0:T(8,128)} async-done(((f32[512,128]{1,0:T(8,128)}), f32[16,128]{1,0:T(8,128)}) %reduce-scatter.8.cloned.1.call-update) | async-done | bytes 8208 | tf_op jit(solution)/shard_map/reduce_scatter | solution.py:157
  (85 shorter events, 12.6 us)
Async XLA Ops:
  7.2 411.6 %copy-start = (bf16[128,384]{1,0:T(8,128)(2,1)S(1)}, bf16[128,384]{1,0:T(8,128)(2,1)}, u32[]{:S(2)}) copy-start(bf16[128,384]{1,0:T(8,128)(2,1)} %param.24) | copy-start | bytes 294916
  7.2 262.7 %reduce-scatter.4.cloned.1.call-start = ((), (), s32[]{:S(2)}) async-start(), calls=%async_computation.3 | async-start | bytes 2162688 | tf_op jit(solution)/shard_map/reduce_scatter | solution.py:132
  10.9 3.1 copy-start.2
  18.1 3.1 copy-start.2
  25.2 3.1 copy-start.2
  32.4 3.1 copy-start.2
  37.2 0.7 copy-start.10
  46.7 1.4 copy-start.1
  46.7 288.0 %copy-start.8 = (s32[128,8]{0,1:T(8,128)S(1)}, s32[128,8]{0,1:T(8,128)}, u32[]{:S(2)}) copy-start(s32[128,8]{0,1:T(8,128)} %param.20) | copy-start | bytes 12292
  46.7 288.2 %copy-start.9 = (s32[128,8]{0,1:T(8,128)S(1)}, s32[128,8]{0,1:T(8,128)}, u32[]{:S(2)}) copy-start(s32[128,8]{0,1:T(8,128)} %param.21) | copy-start | bytes 12292
  46.7 288.3 %copy-start.5 = (bf16[128,512]{1,0:T(8,128)(2,1)S(1)}, bf16[128,512]{1,0:T(8,128)(2,1)}, u32[]{:S(2)}) copy-start(bf16[128,512]{1,0:T(8,128)(2,1)} %param.23) | copy-start | bytes 393220
  46.7 288.9 %copy-start.6 = (bf16[128,256]{1,0:T(8,128)(2,1)S(1)}, bf16[128,256]{1,0:T(8,128)(2,1)}, u32[]{:S(2)}) copy-start(bf16[128,256]{1,0:T(8,128)(2,1)} %param.25) | copy-start | bytes 196612
  48.1 285.1 %all-reduce.2.cloned.1.call-start = ((), (), s32[]{:S(2)}) async-start(), calls=%async_computation.4 | async-start | bytes 131072 | tf_op jit(solution)/shard_map/psum | solution.py:133
  269.9 143.9 %all-gather.3.cloned.1.call-start = ((), (), s32[]{:S(2)}) async-start(), calls=%async_computation.5 | async-start | bytes 1081344 | tf_op jit(solution)/shard_map/all_gather | solution.py:136
  334.6 311.5 %reduce-scatter.6.cloned.1.call-start = ((), (), s32[]{:S(2)}) async-start(), calls=%async_computation.6 | async-start | bytes 2162688 | tf_op jit(solution)/shard_map/reduce_scatter | solution.py:144
  418.1 0.9 copy-start.3
  418.1 0.9 copy-start.7
  418.1 0.9 copy-start.11
  418.1 1.1 copy-start.4
  429.9 293.4 %all-gather.5.cloned.1.call-start = ((), (), s32[]{:S(2)}) async-start(), calls=%async_computation.7 | async-start | bytes 1081344 | tf_op jit(solution)/shard_map/all_gather | solution.py:151
  647.8 298.1 %reduce-scatter.8.cloned.1.call-start = ((), (), s32[]{:S(2)}) async-start(), calls=%async_computation.8 | async-start | bytes 270336 | tf_op jit(solution)/shard_map/reduce_scatter | solution.py:157
Sparse Core Ops, SparseCore 0:
  48.2 221.6 reduce-scatter.3
  272.2 60.8 all-reduce.1
  336.3 77.4 all-gather.2
  430.0 216.0 reduce-scatter.5
  648.6 74.6 all-gather.4
  732.3 213.5 reduce-scatter.7
where the time goes:
time: 954 us; the launch traced here: 953 us
  waiting for transfers between devices  868 us (91%)
  matrix products  30 us (3%)
  local copies, waits for them, and re-layouts  20.8 us (2%)
  other arithmetic  18.9 us (2%)
  between operations  15.1 us (2%)
    reduce_scatter x1, waiting for transfers between devices, body(): lax.psum_scatter(partial_value, 'dom', scatter_dimension=0, tiled=True)  222 us
    reduce_scatter x1, waiting for transfers between devices, body(): lax.psum_scatter(rows_in_window(flat_contrib, flat_targets, lax.axis_size...  216 us
    reduce_scatter x1, waiting for transfers between devices, body(): lax.psum_scatter(jnp.einsum('bif,bih->fh', aggregated, picked_grads, pref...  214 us
    all_gather x1, waiting for transfers between devices, body(): all_states = lax.all_gather(states, 'dom', axis=0, tiled=True)  77.3 us
    all_gather x1, waiting for transfers between devices, body(): all_grads = lax.all_gather(first_grad, 'dom', axis=0, tiled=True)  75.4 us
    psum x1, waiting for transfers between devices, body(): first = lax.psum(owned, 'cuts')  63.2 us
  transfers between devices with their start and end apart: 6, of which 6 were waited for; matrix products, arithmetic and copies ran while one was open for 0% of the time, Pallas kernels for 0%

commit v1 on v0

--- a/solution.py
+++ b/solution.py
@@ -130,7 +130,10 @@
         projected, blk_dst, num_segments=total_rows // block_rows
     ).reshape(total_rows, hidden)
     owned = lax.psum_scatter(partial_value, "dom", scatter_dimension=0, tiled=True)
-    first = lax.psum(owned, "cuts")
+    peers, first = (lax.axis_size("cuts"), owned)
+    for far in [1 << k for k in range(peers.bit_length() - 1)]:
+        route = [(i, i ^ far) for i in range(peers)]
+        first = first + lax.ppermute(first, "cuts", route)
     state_exact = jnp.tanh(first)
     states = state_exact.astype(jnp.bfloat16)
     all_states = lax.all_gather(states, "dom", axis=0, tiled=True)

time: 954 us -> 897 us (0.940)
  waiting for transfers between devices: 868 us -> 809 us
    psum x1 -> x0, waiting for transfers between devices: 63.2 us -> none  [body(): first = lax.psum(owned, 'cuts')]
  transfers between devices with their start and end apart: 6 -> 8, of which waited for: 6 -> 8; matrix products, arithmetic and copies ran while one was open for 0% -> 0% of each run, Pallas kernels for 0% -> 0%
where the time goes in v1:
time: 897 us
  waiting for transfers between devices  809 us (90%)
  matrix products  30.1 us (3%)
  local copies, waits for them, and re-layouts  20.8 us (2%)
  other arithmetic  19 us (2%)
  between operations  14.7 us (2%)
    reduce_scatter x1, waiting for transfers between devices, body(): lax.psum_scatter(partial_value, 'dom', scatter_dimension=0, tiled=True)  222 us
    reduce_scatter x1, waiting for transfers between devices, body(): lax.psum_scatter(rows_in_window(flat_contrib, flat_targets, lax.axis_size...  216 us
    reduce_scatter x1, waiting for transfers between devices, body(): lax.psum_scatter(jnp.einsum('bif,bih->fh', aggregated, picked_grads, pref...  214 us
    all_gather x1, waiting for transfers between devices, body(): all_grads = lax.all_gather(first_grad, 'dom', axis=0, tiled=True)  75.2 us
    all_gather x1, waiting for transfers between devices, body(): all_states = lax.all_gather(states, 'dom', axis=0, tiled=True)  72.8 us
  transfers between devices with their start and end apart: 8, of which 8 were waited for; matrix products, arithmetic and copies ran while one was open for 0% of the time, Pallas kernels for 0%

profile of v1, /device:TPU:8, one launch (start us, length us, event | category | flops | bytes accessed | tf_op | source)
XLA Modules:
  0.0 896.7 jit_solution(5829891584928711377)
XLA Ops:
  8.6 28.6 %while.12 = (s32[]{:T(128)}, bf16[4,16,128,512]{3,2,1,0:T(8,128)(2,1)}, f32[4,16,128,128]{3,2,1,0:T(8,128)}, bf16[4,16,128,128]{3,2,1,0:T(8,128)(2,1)}, s32[4,16...) while((s32[]{:T(128)}, ...), condition=%wide.region_1.2_spmd, body=%wide.region_0.1_spmd.sunk | while | flops 538182720 | bytes 14817201 | solution.py:119
  8.7 2.3 gather_fusion
  11.0 3.1 bitcast_dynamic-update-slice_fusion.2
  14.1 1.8 fusion.100
  15.9 2.3 gather_fusion
  18.2 3.1 bitcast_dynamic-update-slice_fusion.2
  23.0 2.3 gather_fusion
  25.3 3.1 bitcast_dynamic-update-slice_fusion.2
  30.1 2.3 gather_fusion
  32.4 3.1 bitcast_dynamic-update-slice_fusion.2
  35.5 1.7 fusion.100
  37.9 8.8 scatter_fusion
  48.2 221.8 %reduce-scatter.4.cloned.1.call-done = f32[128,128]{1,0:T(8,128)} async-done(((f32[4096,128]{1,0:T(8,128)}), f32[128,128]{1,0:T(8,128)}) %reduce-scatter.4.cloned.1.call-update) | async-done | bytes 65552 | tf_op jit(solution)/shard_map/reduce_scatter | solution.py:132
  272.9 3.7 collective-permute-done.1
  276.7 2.2 collective-permute-start.2
  278.9 3.6 collective-permute-done.2
  285.1 72.8 %all-gather.3.cloned.1.call-done = bf16[4096,128]{1,0:T(8,128)(2,1)} async-done(((bf16[128,128]{1,0:T(8,128)(2,1)}), bf16[4096,128]{1,0:T(8,128)(2,1)}) %all-gather.3.cloned.1.call-update) | async-done | bytes 1048592 | tf_op jit(solution)/shard_map/all_gather | solution.py:139
  357.9 4.2 gather_fusion.1
  365.3 7.1 scatter_custom_fusion.1
  374.0 216.3 %reduce-scatter.6.cloned.1.call-done = f32[128,128]{1,0:T(8,128)} async-done(((f32[4096,128]{1,0:T(8,128)}), f32[128,128]{1,0:T(8,128)}) %reduce-scatter.6.cloned.1.call-update) | async-done | bytes 65552 | tf_op jit(solution)/shard_map/reduce_scatter | solution.py:147
  592.3 75.2 %all-gather.5.cloned.1.call-done = bf16[4096,128]{1,0:T(8,128)(2,1)} async-done(((bf16[128,128]{1,0:T(8,128)(2,1)}), bf16[4096,128]{1,0:T(8,128)(2,1)}) %all-gather.5.cloned.1.call-update) | async-done | bytes 1048592 | tf_op jit(solution)/shard_map/all_gather | solution.py:154
  667.5 2.2 gather_fusion.2
  669.7 6.7 fusion.12
  676.4 213.7 %reduce-scatter.8.cloned.1.call-done = f32[16,128]{1,0:T(8,128)} async-done(((f32[512,128]{1,0:T(8,128)}), f32[16,128]{1,0:T(8,128)}) %reduce-scatter.8.cloned.1.call-update) | async-done | bytes 8208 | tf_op jit(solution)/shard_map/reduce_scatter | solution.py:160
  (88 shorter events, 18.3 us)
Async XLA Ops:
  7.2 355.7 %copy-start = (bf16[128,384]{1,0:T(8,128)(2,1)S(1)}, bf16[128,384]{1,0:T(8,128)(2,1)}, u32[]{:S(2)}) copy-start(bf16[128,384]{1,0:T(8,128)(2,1)} %param.24) | copy-start | bytes 294916
  7.2 262.8 %reduce-scatter.4.cloned.1.call-start = ((), (), s32[]{:S(2)}) async-start(), calls=%async_computation.3 | async-start | bytes 2162688 | tf_op jit(solution)/shard_map/reduce_scatter | solution.py:132
  10.9 3.1 copy-start.2
  18.2 3.1 copy-start.2
  25.3 3.1 copy-start.2
  32.4 3.1 copy-start.2
  37.3 0.7 copy-start.9
  46.7 1.4 copy-start.1
  46.7 236.5 %copy-start.7 = (s32[128,8]{0,1:T(8,128)S(1)}, s32[128,8]{0,1:T(8,128)}, u32[]{:S(2)}) copy-start(s32[128,8]{0,1:T(8,128)} %param.20) | copy-start | bytes 12292
  46.8 236.7 %copy-start.8 = (s32[128,8]{0,1:T(8,128)S(1)}, s32[128,8]{0,1:T(8,128)}, u32[]{:S(2)}) copy-start(s32[128,8]{0,1:T(8,128)} %param.21) | copy-start | bytes 12292
  46.8 236.8 %copy-start.5 = (bf16[128,512]{1,0:T(8,128)(2,1)S(1)}, bf16[128,512]{1,0:T(8,128)(2,1)}, u32[]{:S(2)}) copy-start(bf16[128,512]{1,0:T(8,128)(2,1)} %param.23) | copy-start | bytes 393220
  46.8 237.4 %copy-start.4 = (bf16[128,256]{1,0:T(8,128)(2,1)S(1)}, bf16[128,256]{1,0:T(8,128)(2,1)}, u32[]{:S(2)}) copy-start(bf16[128,256]{1,0:T(8,128)(2,1)} %param.25) | copy-start | bytes 196612
  48.1 309.8 %all-gather.3.cloned.1.call-start = ((), (), s32[]{:S(2)}) async-start(), calls=%async_computation.4 | async-start | bytes 1081344 | tf_op jit(solution)/shard_map/all_gather | solution.py:139
  270.0 1.5 collective-permute-start
  272.3 4.3 collective-permute-start.1
  276.7 5.9 collective-permute-start.2
  283.2 307.2 %reduce-scatter.6.cloned.1.call-start = ((), (), s32[]{:S(2)}) async-start(), calls=%async_computation.5 | async-start | bytes 2162688 | tf_op jit(solution)/shard_map/reduce_scatter | solution.py:147
  362.2 0.9 copy-start.3
  362.2 0.9 copy-start.6
  362.2 0.9 copy-start.10
  374.0 293.5 %all-gather.5.cloned.1.call-start = ((), (), s32[]{:S(2)}) async-start(), calls=%async_computation.6 | async-start | bytes 1081344 | tf_op jit(solution)/shard_map/all_gather | solution.py:154
  592.0 298.1 %reduce-scatter.8.cloned.1.call-start = ((), (), s32[]{:S(2)}) async-start(), calls=%async_computation.7 | async-start | bytes 270336 | tf_op jit(solution)/shard_map/reduce_scatter | solution.py:160
Sparse Core Ops, SparseCore 0:
  48.2 221.6 reduce-scatter.3
  283.3 74.5 all-gather.2
  374.1 216.2 reduce-scatter.5
  592.8 74.6 all-gather.4
  676.5 213.5 reduce-scatter.7
